TPU v7x, 32 devices: a whole 2x2x4 slice. The times are simulated.
32 devices in a mesh: parts: 2 (over y), tm: 8 (over z, x), band: 2 (over core).
Axes of the slice: x: 2, y: 2, z: 4, core: 2. Of those that a mesh axis runs over, the one named last changes fastest.
Arguments:
- query_tokens: bfloat16 [16, 8, 32, 2240], P(('parts', 'tm'), 'band'), parts along dimension 0, may hold values from -6 to 6
- key_tokens: bfloat16 [16, 8, 32, 2240], P(('parts', 'tm'), 'band'), parts along dimension 0, may hold values from -6 to 6
- value_tokens: bfloat16 [16, 8, 32, 2240], P(('parts', 'tm'), 'band'), parts along dimension 0, may hold values from -14 to 14
- norm_gain: float32 [2240], replicated, may hold values from 0.1 to 1.9
- out_weight: bfloat16 [2, 8, 313600], P('band', 'tm'), may hold values from -0.125 to 0.125
Outputs:
- block_out: bfloat16 [16, 8, 32, 2240], P(('parts', 'tm'), 'band'), parts along dimension 0
There are 2 independent parts, one for each index of `parts`. A program takes and returns all parts, laid end to end along the dimension named above; an argument that names none is the same for every part. Nothing has to cross between parts.
All inputs are finite; a program needn't handle non-finite values.
Results may differ from a plain program's by a relative error of at most 0.0049.
Values may be sent and summed in bfloat16 or wider, within the bound.
No kernel may reach another device: no remote copies, remote signals or barrier semaphores. Data moves between devices by JAX's collectives and lax.ppermute only.
A program may use at most 128 MiB of HBM per device.

v0:
```python
import jax
import jax.numpy as jnp
from jax import lax
from jax.sharding import PartitionSpec as P

HEADS = 70
HD = 32
norm_epsilon = 1e-06
read_epsilon = 1e-06


def entering(x, axis, combine, identity):
    peers, place = (lax.axis_size(axis), lax.axis_index(axis))
    everything = jax.tree.map(lambda part: lax.all_gather(part, axis), x)
    start = jax.tree.map(
        lambda part, zero: jnp.broadcast_to(jnp.asarray(zero, part.dtype), part.shape), x, identity
    )

    def hop(k, before):
        reached = k < place
        new = combine(before, jax.tree.map(lambda part: part[k], everything))
        return jax.tree.map(lambda a, b: jnp.where(reached, a, b), new, before)

    return lax.fori_loop(0, peers, hop, start)


def add_pair(earlier, later):
    return (earlier[0] + later[0], earlier[1] + later[1])


def body(query_tokens, key_tokens, value_tokens, norm_gain, out_weight):
    frames, rows, width, depth = query_tokens.shape
    key_relu = jax.nn.relu(key_tokens).reshape(frames, rows * width, HEADS, HD)
    value_heads = value_tokens.reshape(frames, rows * width, HEADS, HD)
    part_state = jnp.einsum(
        "fthd,fthe->fhde", key_relu, value_heads, preferred_element_type=jnp.float32
    ).reshape(frames, HEADS, HD * HD)
    part_norm = jnp.sum(key_relu, axis=1, dtype=jnp.float32)
    state_sum, norm_sum = lax.psum((part_state, part_norm), "band")
    local_state = jnp.cumsum(state_sum, axis=0)
    local_norm = jnp.cumsum(norm_sum, axis=0)
    before = entering(
        (local_state[-1], local_norm[-1]),
        "tm",
        add_pair,
        (jnp.zeros_like(local_state[-1]), jnp.zeros_like(local_norm[-1])),
    )
    prefix_state = local_state + before[0]
    prefix_norm = local_norm + before[1]
    query_relu = jax.nn.relu(query_tokens.astype(jnp.float32)).reshape(
        frames, rows * width, HEADS, HD
    )
    numer = jnp.einsum(
        "fthd,fhde->fthe",
        query_relu,
        prefix_state.reshape(frames, HEADS, HD, HD),
        precision=lax.Precision.HIGHEST,
    )
    denom = (
        jnp.einsum("fthd,fhd->fth", query_relu, prefix_norm, precision=lax.Precision.HIGHEST)
        + read_epsilon
    )
    reads = (numer / denom[:, :, :, None]).reshape(frames * rows * width, depth)
    square = jnp.mean(reads * reads, axis=-1, keepdims=True)
    normed = (reads * lax.rsqrt(square + norm_epsilon) * norm_gain).astype(jnp.bfloat16)
    gathered = lax.all_gather(out_weight, "tm", axis=1, tiled=True)
    rows_half = gathered.reshape(-1, depth)
    result = jnp.dot(
        normed,
        lax.all_gather(rows_half, "band", axis=0, tiled=True),
        preferred_element_type=jnp.float32,
    )
    return result.astype(jnp.bfloat16).reshape(frames, rows, width, depth)


def solution(mesh):
    in_specs = (
        P(("parts", "tm"), "band", None, None),
        P(("parts", "tm"), "band", None, None),
        P(("parts", "tm"), "band", None, None),
        P(),
        P("band", "tm", None),
    )
    out_specs = P(("parts", "tm"), "band", None, None)
    return jax.shard_map(body, mesh=mesh, in_specs=in_specs, out_specs=out_specs, check_vma=False)
```

profile of v0, /device:TPU:0, one launch (start us, length us, event | category | flops | bytes accessed | tf_op | source)
XLA Modules:
  0.0 356.1 jit_solution(12308929848867415624)
XLA Ops:
  7.4 0.0 all-reduce.2.cloned.1.call-start
  7.4 1.1 broadcast_maximum_fusion
  8.5 0.0 copy-start.4
  8.5 2.0 reshape.61
  10.5 0.0 copy-done.4
  10.5 3.0 reshape.62
  13.4 2.4 fusion
  15.9 1.6 copy.32
  17.4 0.0 all-reduce.2.cloned.1.call-update
  17.5 0.0 all-gather.6.cloned.1.call-start
  17.5 0.5 all-gather.6.cloned.1.call-update
  18.0 0.0 all-gather.4.cloned.1.call-start
  18.1 20.8 %all-reduce.2.cloned.1.call-done = f32[1,70,1024]{1,2,0:T(8,128)} async-done(((f32[1,70,1024]{1,2,0:T(8,128)}), f32[1,70,1024]{1,2,0:T(8,128)}) %all-reduce.2.cloned.1.call-update) | async-done | bytes 286736 | tf_op jit(solution)/shard_map/psum | solution.py:39
  38.9 2.0 copy.33
  40.9 0.0 all-gather.4.cloned.1.call-update
  40.9 0.0 all-gather.8.cloned.1.call-start
  41.0 126.2 %all-gather.6.cloned.1.call-done = bf16[1,8,313600]{2,0,1:T(2,128)(2,1)} async-done(((bf16[1,1,313600]{2,0,1:T(2,128)(2,1)}), bf16[1,8,313600]{2,0,1:T(2,128)(2,1)}) %all-gather.6.cloned.1.call-update) | async-done | bytes 5017616 | tf_op jit(solution)/shard_map/all_gather | solution.py:66
  167.2 90.6 %reduce.3 = bf16[8,313600]{1,0:T(8,128)(2,1)} reduce(bf16[1,8,313600]{2,0,1:T(2,128)(2,1)} %all-gather.6.cloned.1.call-done, bf16[]{:T(256)} %constant.55), dimensions={0}, to_apply=%all_gather.14.reduce_sub_computation | reduce | bytes 10035202 | tf_op jit(solution)/shard_map/all_gather | solution.py:66
  257.7 12.1 %reshape.73 = bf16[2508800]{0:T(1024)(128)(2,1)} reshape(bf16[8,313600]{1,0:T(8,128)(2,1)} %reduce.3) | data formatting | bytes 10035200
  269.8 9.4 %reshape.68 = bf16[1120,2240]{1,0:T(8,128)(2,1)} reshape(bf16[2508800]{0:T(1024)(128)(2,1)} %reshape.73) | data formatting | bytes 10035200 | tf_op jit(solution)/shard_map/reshape | solution.py:67
  279.3 0.0 copy-start
  279.3 0.0 all-gather.8.cloned.1.call-update
  279.3 0.0 copy-start.3
  279.3 1.0 copy-done
  280.3 0.1 convert_reduce_fusion
  280.5 0.1 reduce_sum.21
  280.6 3.5 psum.15
  284.0 0.1 copy.34
  284.1 0.0 copy-done.3
  284.1 0.1 convert_maximum_fusion
  284.2 3.7 %reshape.65 = f32[128,70,32]{2,1,0:T(8,128)} reshape(f32[1,4,32,2240]{3,2,1,0:T(8,128)S(1)} %convert_maximum_fusion) | data formatting | bytes 2293760 | tf_op jit(solution)/shard_map/reshape.5
  287.9 4.7 %copy.38 = f32[128,70,32]{0,2,1:T(8,128)S(1)} copy(f32[128,70,32]{2,1,0:T(8,128)} %reshape.65) | data formatting | bytes 2293760 | tf_op jit(solution)/shard_map/reshape.5
  292.6 30.5 %all_gather.13 = f32[8,70,32]{1,2,0:T(8,128)S(1)} all-gather(f32[1,70,32]{1,2,0:T(8,128)S(1)} %copy.34), channel_id=1, replica_groups=mesh['parts'=2,'tm'=8,'band'=2] {'tm'}, dimensions={0}, use_global_device_ids=true | all-gather | bytes 80640 | tf_op jit(solution)/shard_map/all_gather | solution.py:14
  323.1 0.0 all-gather.4.cloned.1.call-done
  323.1 10.0 %while.16 = (s32[]{:T(128)}, f32[70,1024]{1,0:T(8,128)S(1)}, f32[70,32]{1,0:T(8,128)S(1)}, s32[]{:T(128)}, f32[8,70,1024]{2,1,0:T(8,128)}, /*index=5*/f32[8,70,32]{1,2,0:T(8,128)S(1)}, s32[]{:T(128)}, s32[]{:T(128)}) while((s32[]{:T(128)}, f32[70,1024]{1,0:T(8,128)S(1)}, f32[70,32]{1,0:T(8,128)S(1)}, s32[]{:T(128)}, ...), condition=%wide.region_4.5_spmd.clone, body=%wide.region_3.4_spmd.clone.sunk | while | flops 221764 | bytes 922995 | solution.py:24
  323.3 1.1 add_select_fusion.4
  324.4 0.1 copy.52
  324.5 1.1 add_select_fusion.4
  325.6 0.1 copy.52
  325.8 1.1 add_select_fusion.4
  326.9 0.1 copy.52
  327.0 1.1 add_select_fusion.4
  328.1 0.1 copy.52
  328.2 1.1 add_select_fusion.4
  329.3 0.1 copy.52
  329.4 1.1 add_select_fusion.4
  330.5 0.1 copy.52
  330.6 1.1 add_select_fusion.4
  331.7 0.1 copy.52
  331.9 1.1 add_select_fusion.4
  333.0 0.1 copy.52
  333.1 0.0 copy-start.1
  333.1 0.2 copy.36
  333.3 0.8 copy-done.1
  334.1 0.1 bitcast_add_fusion
  334.2 2.0 copy.37
  336.2 1.0 fusion.8
  337.2 0.2 copy-done.2
  337.4 1.5 multiply_reduce_fusion
  338.9 0.0 copy-done.5
  338.9 0.4 fusion.4
  339.3 0.0 all-gather.8.cloned.1.call-done
  339.3 8.1 %convolution_convert_fusion = bf16[128,2240]{0,1:T(8,128)(2,1)S(1)} fusion(bf16[128,2240]{0,1:T(8,128)(2,1)S(1)} %fusion.4, bf16[2240,2240]{1,0:T(8,128)(2,1)} %all-gather.8.cloned.1.call-done), kind=kOutput, calls=%fused_computation.3 | convolution fusion | flops 1284792320 | bytes 11182080 | tf_op jit(solution)/shard_map/dot_general | solution.py:68
  347.4 1.1 copy.40
  (23 shorter events, 0.2 us)
Async XLA Ops:
  7.4 31.6 %all-reduce.2.cloned.1.call-start = ((), (), s32[]{:S(2)}) async-start(), calls=%async_computation | async-start | bytes 1048576 | tf_op jit(solution)/shard_map/psum | solution.py:39
  8.5 2.0 copy-start.4
  17.5 149.7 %all-gather.6.cloned.1.call-start = ((), (), s32[]{:S(2)}) async-start(), calls=%async_computation.2 | async-start | bytes 11289600 | tf_op jit(solution)/shard_map/all_gather | solution.py:66
  18.0 305.1 %all-gather.4.cloned.1.call-start = ((), (), s32[]{:S(2)}) async-start(), calls=%async_computation.1 | async-start | bytes 2654208 | tf_op jit(solution)/shard_map/all_gather | solution.py:14
  40.9 298.4 %all-gather.8.cloned.1.call-start = ((), (), s32[]{:S(2)}) async-start(), calls=%async_computation.3 | async-start | bytes 15482880 | tf_op jit(solution)/shard_map/all_gather | solution.py:70
  279.3 1.1 copy-start
  279.3 4.8 %copy-start.3 = (bf16[1,4,32,2240]{3,2,1,0:T(8,128)(2,1)S(1)}, bf16[1,4,32,2240]{3,2,1,0:T(8,128)(2,1)}, u32[]{:S(2)}) copy-start(bf16[1,4,32,2240]{3,2,1,0:T(8,128)(2,1)} %param.7) | copy-start | bytes 1720324
  333.1 1.0 copy-start.1
  336.1 1.3 copy-start.2
  337.4 1.5 copy-start.5
Sparse Core Ops, SparseCore 0:
  17.6 21.3 all-reduce.1
Sparse Core Ops, SparseCore 1:
  20.1 147.0 all-gather.5
  169.2 49.8 all-gather.3
  279.4 20.5 all-gather.7
where the time goes:
time: 357 us; the launch traced here: 356 us
  waiting for transfers between devices  148 us (41%)
  other arithmetic  101 us (28%)
  local copies, waits for them, and re-layouts  44.7 us (13%)
  blocking collectives  34 us (10%)
  between operations  15.2 us (4%)
  matrix products  13 us (4%)
    all_gather x1, waiting for transfers between devices, body(): gathered = lax.all_gather(out_weight, 'tm', axis=1, tiled=True)  126 us
    all_gather x1, other arithmetic, body(): gathered = lax.all_gather(out_weight, 'tm', axis=1, tiled=True)  90.6 us
    all_gather x1, blocking collectives, entering(): everything = jax.tree.map(lambda part: lax.all_gather(part, axis), x)  30.5 us
    psum x1, waiting for transfers between devices, body(): state_sum, norm_sum = lax.psum((part_state, part_norm), 'band')  20.8 us
    unnamed x13, local copies, waits for them, and re-layouts  14.1 us
    another operation x4, local copies, waits for them, and re-layouts  13.3 us
    reshape x1, local copies, waits for them, and re-layouts, body(): rows_half = gathered.reshape(-1, depth)  9.45 us
    select_n x16, other arithmetic, hop(): return jax.tree.map(lambda a, b: jnp.where(reached, a, b), new, before)  8.63 us
  transfers between devices with their start and end apart: 4, of which 2 were waited for; matrix products, arithmetic and copies ran while one was open for 39% of the time, Pallas kernels for 0%

commit v1 on v0

--- a/solution.py
+++ b/solution.py
@@ -7,6 +7,16 @@
 HD = 32
 norm_epsilon = 1e-06
 read_epsilon = 1e-06
+
+
+def around_the_ring(x, mesh_axis, dim):
+    devices = lax.axis_size(mesh_axis)
+    held, parts = (x, [x])
+    for _ in range(devices - 1):
+        held = lax.ppermute(held, mesh_axis, [(i, (i + 1) % devices) for i in range(devices)])
+        parts.insert(0, held)
+    flat = jnp.concatenate(parts, axis=dim)
+    return jnp.roll(flat, (lax.axis_index(mesh_axis) + 1) * x.shape[dim], axis=dim)
 
 
 def entering(x, axis, combine, identity):
@@ -63,7 +73,7 @@
     reads = (numer / denom[:, :, :, None]).reshape(frames * rows * width, depth)
     square = jnp.mean(reads * reads, axis=-1, keepdims=True)
     normed = (reads * lax.rsqrt(square + norm_epsilon) * norm_gain).astype(jnp.bfloat16)
-    gathered = lax.all_gather(out_weight, "tm", axis=1, tiled=True)
+    gathered = around_the_ring(out_weight, "tm", 1)
     rows_half = gathered.reshape(-1, depth)
     result = jnp.dot(
         normed,

time: 357 us -> 385 us (1.078); the launches traced: 356 us -> 378 us
  other arithmetic: 101 us -> 10.5 us
  local copies, waits for them, and re-layouts: 44.7 us -> 109 us
  waiting for transfers between devices: 148 us -> 193 us
    ppermute x0 -> x7, waiting for transfers between devices: none -> 174 us  [around_the_ring(): lax.ppermute(held, mesh_axis, [(i, (i + 1) % devices) for i in range(devi...]
    all_gather x1 -> x0, waiting for transfers between devices: 126 us -> none  [body(): gathered = lax.all_gather(out_weight, 'tm', axis=1, tiled=True)]
    all_gather x1 -> x0, other arithmetic: 90.6 us -> none  [body(): gathered = lax.all_gather(out_weight, 'tm', axis=1, tiled=True)]
    concatenate x0 -> x1, local copies, waits for them, and re-layouts: none -> 52.3 us  [around_the_ring(): jnp.roll(flat, (lax.axis_index(mesh_axis) + 1) * x.shape[dim], axis=dim)]
    dynamic_slice x0 -> x1, local copies, waits for them, and re-layouts: none -> 7.4 us  [around_the_ring(): jnp.roll(flat, (lax.axis_index(mesh_axis) + 1) * x.shape[dim], axis=dim)]
    unnamed x13 -> x25, local copies, waits for them, and re-layouts: 14.1 us -> 17.6 us
  transfers between devices with their start and end apart: 4 -> 10, of which waited for: 2 -> 7; matrix products, arithmetic and copies ran while one was open for 39% -> 31% of each run, Pallas kernels for 0% -> 0%
where the time goes in v1:
time: 385 us; the launch traced here: 378 us
  waiting for transfers between devices  193 us (50%)
  local copies, waits for them, and re-layouts  109 us (28%)
  blocking collectives  34.6 us (9%)
  matrix products  14.1 us (4%)
  between operations  13.3 us (3%)
  other arithmetic  10.5 us (3%)
    ppermute x7, waiting for transfers between devices, around_the_ring(): lax.ppermute(held, mesh_axis, [(i, (i + 1) % devices) for i in range(devi...  174 us
    concatenate x1, local copies, waits for them, and re-layouts, around_the_ring(): jnp.roll(flat, (lax.axis_index(mesh_axis) + 1) * x.shape[dim], axis=dim)  52.3 us
    all_gather x1, blocking collectives, entering(): everything = jax.tree.map(lambda part: lax.all_gather(part, axis), x)  30.9 us
    psum x1, waiting for transfers between devices, body(): state_sum, norm_sum = lax.psum((part_state, part_norm), 'band')  19.2 us
    unnamed x25, local copies, waits for them, and re-layouts  17.6 us
    another operation x4, local copies, waits for them, and re-layouts  13.1 us
    reshape x1, local copies, waits for them, and re-layouts, body(): rows_half = gathered.reshape(-1, depth)  9.45 us
    select_n x16, other arithmetic, hop(): return jax.tree.map(lambda a, b: jnp.where(reached, a, b), new, before)  8.68 us
  transfers between devices with their start and end apart: 10, of which 7 were waited for; matrix products, arithmetic and copies ran while one was open for 31% of the time, Pallas kernels for 0%

profile of v1, /device:TPU:0, one launch (start us, length us, event | category | flops | bytes accessed | tf_op | source)
XLA Modules:
  0.0 377.9 jit_solution(11964030976587311869)
XLA Ops:
  6.5 3.0 collective-permute-start
  9.5 30.8 %collective-permute-done = bf16[1,1,313600]{2,1,0:T(2,128)(2,1)S(1)} collective-permute-done((bf16[1,1,313600]{2,1,0:T(2,128)(2,1)}, bf16[1,1,313600]{2,1,0:T(2,128)(2,1)S(1)}, u32[]{:S(2)}, u32[]{:S(2)}) %collective-permute-start) | collective-permute-done | bytes 627232 | tf_op jit(solution)/shard_map/ppermute | solution.py:16
  40.3 1.1 copy-done.1
  41.4 31.4 %collective-permute-done.1 = bf16[1,1,313600]{2,1,0:T(2,128)(2,1)S(1)} collective-permute-done((bf16[1,1,313600]{2,1,0:T(2,128)(2,1)S(1)}, bf16[1,1,313600]{2,1,0:T(2,128)(2,1)S(1)}, u32[]{:S(2)}, u32[]{:S(2)}) %collective-permute-start.1) | collective-permute-done | bytes 627232 | tf_op jit(solution)/shard_map/ppermute | solution.py:16
  72.8 1.1 copy-done.3
  73.9 30.6 %collective-permute-done.2 = bf16[1,1,313600]{2,1,0:T(2,128)(2,1)S(1)} collective-permute-done((bf16[1,1,313600]{2,1,0:T(2,128)(2,1)S(1)}, bf16[1,1,313600]{2,1,0:T(2,128)(2,1)S(1)}, u32[]{:S(2)}, u32[]{:S(2)}) %collective-permute-start.2) | collective-permute-done | bytes 627232 | tf_op jit(solution)/shard_map/ppermute | solution.py:16
  104.5 1.0 copy-done.4
  105.5 29.7 %collective-permute-done.3 = bf16[1,1,313600]{2,1,0:T(2,128)(2,1)S(1)} collective-permute-done((bf16[1,1,313600]{2,1,0:T(2,128)(2,1)S(1)}, bf16[1,1,313600]{2,1,0:T(2,128)(2,1)S(1)}, u32[]{:S(2)}, u32[]{:S(2)}) %collective-permute-start.3) | collective-permute-done | bytes 627232 | tf_op jit(solution)/shard_map/ppermute | solution.py:16
  135.2 1.1 copy-done.5
  136.3 29.0 %collective-permute-done.4 = bf16[1,1,313600]{2,1,0:T(2,128)(2,1)} collective-permute-done((bf16[1,1,313600]{2,1,0:T(2,128)(2,1)S(1)}, bf16[1,1,313600]{2,1,0:T(2,128)(2,1)}, u32[]{:S(2)}, u32[]{:S(2)}) %collective-permute-start.4) | collective-permute-done | bytes 627232 | tf_op jit(solution)/shard_map/ppermute | solution.py:16
  165.3 1.1 broadcast_maximum_fusion
  166.4 0.0 copy-start.10
  166.4 2.0 reshape.61
  168.4 3.0 reshape.62
  171.4 22.3 %collective-permute-done.5 = bf16[1,1,313600]{2,1,0:T(2,128)(2,1)} collective-permute-done((bf16[1,1,313600]{2,1,0:T(2,128)(2,1)}, bf16[1,1,313600]{2,1,0:T(2,128)(2,1)}, u32[]{:S(2)}, u32[]{:S(2)}) %collective-permute-start.5) | collective-permute-done | bytes 627232 | tf_op jit(solution)/shard_map/ppermute | solution.py:16
  193.6 3.4 fusion
  197.1 2.8 copy.21
  199.9 0.0 all-reduce.2.cloned.1.call-update
  199.9 0.0 all-gather.3.cloned.1.call-start
  200.0 19.2 %all-reduce.2.cloned.1.call-done = f32[1,70,1024]{1,2,0:T(8,128)} async-done(((f32[1,70,1024]{1,2,0:T(8,128)}), f32[1,70,1024]{1,2,0:T(8,128)}) %all-reduce.2.cloned.1.call-update) | async-done | bytes 286736 | tf_op jit(solution)/shard_map/psum | solution.py:49
  219.1 2.0 copy.22
  221.1 0.0 all-gather.3.cloned.1.call-update
  221.1 0.2 all-gather.5.cloned.1.call-start
  221.4 52.3 %concatenate.6 = bf16[1,16,313600]{2,1,0:T(8,128)(2,1)} concatenate(bf16[1,1,313600]{2,1,0:T(2,128)(2,1)} %collective-permute-done.6, bf16[1,1,313600]{2,1,0:T(2,128)(2,1)} %collective-permute-done.5, bf16[1,1,313600]{2,1,0:T(2,128)(2,1)} %collective-permute-done.4, bf16[1,1,313600]{2,1,0:T(2,128)(2,1)} %copy-done.5, bf16[1,1,313600]{2,1,0:T(2,128)(2,1)} %copy-done.4, ...), dimensions={1} | concatenate | bytes 20070400 | tf_op jit(solution)/shard_map/jit(_roll_dynamic)/concatenate | solution.py:19
  273.7 7.4 %constant_dynamic-slice_fusion.1 = bf16[1,8,313600]{2,1,0:T(8,128)(2,1)} fusion(bf16[1,16,313600]{2,1,0:T(8,128)(2,1)} %concatenate.6, s32[]{:T(128)S(6)} %select_n.52), kind=kLoop, calls=%fused_computation.24 | loop fusion | bytes 10035204 | tf_op jit(solution)/shard_map/jit(_roll_dynamic)/dynamic_slice | solution.py:19
  281.1 12.1 %reshape.72 = bf16[2508800]{0:T(1024)(128)(2,1)} reshape(bf16[1,8,313600]{2,1,0:T(8,128)(2,1)} %constant_dynamic-slice_fusion.1) | data formatting | bytes 10035200
  293.2 9.4 %reshape.68 = bf16[1120,2240]{1,0:T(8,128)(2,1)} reshape(bf16[2508800]{0:T(1024)(128)(2,1)} %reshape.72) | data formatting | bytes 10035200 | tf_op jit(solution)/shard_map/reshape | solution.py:77
  302.6 0.0 all-gather.5.cloned.1.call-update
  302.7 1.0 copy-done.6
  303.7 0.1 convert_reduce_fusion
  303.8 0.1 reduce_sum.21
  303.9 3.8 psum.15
  307.7 0.1 copy.23
  307.7 0.1 convert_maximum_fusion
  307.8 3.4 reshape.65
  311.2 4.9 %copy.27 = f32[128,70,32]{0,2,1:T(8,128)S(1)} copy(f32[128,70,32]{2,1,0:T(8,128)} %reshape.65) | data formatting | bytes 2293760 | tf_op jit(solution)/shard_map/reshape.5
  316.1 30.9 %all_gather.10 = f32[8,70,32]{1,2,0:T(8,128)S(1)} all-gather(f32[1,70,32]{1,2,0:T(8,128)S(1)} %copy.23), channel_id=1, replica_groups=mesh['parts'=2,'tm'=8,'band'=2] {'tm'}, dimensions={0}, use_global_device_ids=true | all-gather | bytes 80640 | tf_op jit(solution)/shard_map/all_gather | solution.py:24
  347.0 9.8 %while.16 = (s32[]{:T(128)}, f32[70,1024]{1,0:T(8,128)S(1)}, f32[70,32]{1,0:T(8,128)S(1)}, s32[]{:T(128)}, f32[8,70,1024]{2,1,0:T(8,128)}, /*index=5*/f32[8,70,32]{1,2,0:T(8,128)S(1)}, s32[]{:T(128)}, s32[]{:T(128)}) while((s32[]{:T(128)}, f32[70,1024]{1,0:T(8,128)S(1)}, f32[70,32]{1,0:T(8,128)S(1)}, s32[]{:T(128)}, ...), condition=%wide.region_4.5_spmd.clone, body=%wide.region_3.4_spmd.clone.sunk | while | flops 221764 | bytes 922995 | solution.py:34
  347.0 1.1 add_select_fusion.4
  348.1 0.1 copy.40
  348.3 1.1 add_select_fusion.4
  349.4 0.1 copy.40
  349.5 1.1 add_select_fusion.4
  350.6 0.1 copy.40
  350.7 1.1 add_select_fusion.4
  351.8 0.1 copy.40
  351.9 1.1 add_select_fusion.4
  353.0 0.1 copy.40
  353.2 1.1 add_select_fusion.4
  354.2 0.1 copy.40
  354.4 1.1 add_select_fusion.4
  355.5 0.1 copy.40
  355.6 1.1 add_select_fusion.4
  356.7 0.1 copy.40
  356.8 0.2 copy.25
  357.0 0.1 bitcast_add_fusion
  357.1 1.9 copy.26
  359.0 1.0 fusion.8
  360.1 0.2 copy-done.8
  360.3 1.5 multiply_reduce_fusion
  361.8 0.4 fusion.4
  362.1 0.0 all-gather.5.cloned.1.call-done
  362.2 8.1 %convolution_convert_fusion = bf16[128,2240]{0,1:T(8,128)(2,1)S(1)} fusion(bf16[128,2240]{0,1:T(8,128)(2,1)S(1)} %fusion.4, bf16[2240,2240]{1,0:T(8,128)(2,1)} %all-gather.5.cloned.1.call-done), kind=kOutput, calls=%fused_computation.3 | convolution fusion | flops 1284792320 | bytes 11182080 | tf_op jit(solution)/shard_map/dot_general | solution.py:78
  370.3 1.1 copy.28
  (47 shorter events, 0.2 us)
Async XLA Ops:
  6.5 212.6 %all-reduce.2.cloned.1.call-start = ((), (), s32[]{:S(2)}) async-start(), calls=%async_computation | async-start | bytes 1048576 | tf_op jit(solution)/shard_map/psum | solution.py:49
  6.5 33.8 %collective-permute-start = (bf16[1,1,313600]{2,1,0:T(2,128)(2,1)}, bf16[1,1,313600]{2,1,0:T(2,128)(2,1)S(1)}, u32[]{:S(2)}, u32[]{:S(2)}) collective-permute-start(bf16[1,1,313600]{2,1,0:T(2,128)(2,1)} %param.11), channel_id=1, source_target_pairs={{0,2},{2,4},{4,6},{6,8},{8,10},{10,12},{12,14},{14,0},{1,3},{3,5},... | collective-permute-start | bytes 1881608 | tf_op jit(solution)/shard_map/ppermute | solution.py:16
  40.3 1.1 copy-start.1
  41.4 31.4 %collective-permute-start.1 = (bf16[1,1,313600]{2,1,0:T(2,128)(2,1)S(1)}, bf16[1,1,313600]{2,1,0:T(2,128)(2,1)S(1)}, u32[]{:S(2)}, u32[]{:S(2)}) collective-permute-start(bf16[1,1,313600]{2,1,0:T(2,128)(2,1)S(1)} %collective-permute-done), channel_id=1, source_target_pairs={{0,2},{2,4},{4,6},{6,8},{8,10},{10,12},{12,14},{14,0},{1,3},{3,5},... | collective-permute-start | bytes 1881608 | tf_op jit(solution)/shard_map/ppermute | solution.py:16
  72.8 1.1 copy-start.3
  73.9 30.6 %collective-permute-start.2 = (bf16[1,1,313600]{2,1,0:T(2,128)(2,1)S(1)}, bf16[1,1,313600]{2,1,0:T(2,128)(2,1)S(1)}, u32[]{:S(2)}, u32[]{:S(2)}) collective-permute-start(bf16[1,1,313600]{2,1,0:T(2,128)(2,1)S(1)} %collective-permute-done.1), channel_id=1, source_target_pairs={{0,2},{2,4},{4,6},{6,8},{8,10},{10,12},{12,14},{14,0},{1,3},{3,5},... | collective-permute-start | bytes 1881608 | tf_op jit(solution)/shard_map/ppermute | solution.py:16
  104.5 1.1 copy-start.4
  105.5 29.7 %collective-permute-start.3 = (bf16[1,1,313600]{2,1,0:T(2,128)(2,1)S(1)}, bf16[1,1,313600]{2,1,0:T(2,128)(2,1)S(1)}, u32[]{:S(2)}, u32[]{:S(2)}) collective-permute-start(bf16[1,1,313600]{2,1,0:T(2,128)(2,1)S(1)} %collective-permute-done.2), channel_id=1, source_target_pairs={{0,2},{2,4},{4,6},{6,8},{8,10},{10,12},{12,14},{14,0},{1,3},{3,5},... | collective-permute-start | bytes 1881608 | tf_op jit(solution)/shard_map/ppermute | solution.py:16
  135.2 1.1 copy-start.5
  136.3 29.0 %collective-permute-start.4 = (bf16[1,1,313600]{2,1,0:T(2,128)(2,1)S(1)}, bf16[1,1,313600]{2,1,0:T(2,128)(2,1)}, u32[]{:S(2)}, u32[]{:S(2)}) collective-permute-start(bf16[1,1,313600]{2,1,0:T(2,128)(2,1)S(1)} %collective-permute-done.3), channel_id=1, source_target_pairs={{0,2},{2,4},{4,6},{6,8},{8,10},{10,12},{12,14},{14,0},{1,3},{3,5},... | collective-permute-start | bytes 1881608 | tf_op jit(solution)/shard_map/ppermute | solution.py:16
  165.3 28.3 %collective-permute-start.5 = (bf16[1,1,313600]{2,1,0:T(2,128)(2,1)}, bf16[1,1,313600]{2,1,0:T(2,128)(2,1)}, u32[]{:S(2)}, u32[]{:S(2)}) collective-permute-start(bf16[1,1,313600]{2,1,0:T(2,128)(2,1)} %collective-permute-done.4), channel_id=1, source_target_pairs={{0,2},{2,4},{4,6},{6,8},{8,10},{10,12},{12,14},{14,0},{1,3},{3,5},... | collective-permute-start | bytes 1881608 | tf_op jit(solution)/shard_map/ppermute | solution.py:16
  166.4 2.0 copy-start.10
  193.6 27.7 %collective-permute-start.6 = (bf16[1,1,313600]{2,1,0:T(2,128)(2,1)}, bf16[1,1,313600]{2,1,0:T(2,128)(2,1)}, u32[]{:S(2)}, u32[]{:S(2)}) collective-permute-start(bf16[1,1,313600]{2,1,0:T(2,128)(2,1)} %collective-permute-done.5), channel_id=1, source_target_pairs={{0,2},{2,4},{4,6},{6,8},{8,10},{10,12},{12,14},{14,0},{1,3},{3,5},... | collective-permute-start | bytes 1881608 | tf_op jit(solution)/shard_map/ppermute | solution.py:16
  197.1 24.3 %copy-start.2 = (bf16[1,1,313600]{2,1,0:T(2,128)(2,1)S(1)}, bf16[1,1,313600]{2,1,0:T(2,128)(2,1)}, u32[]{:S(2)}) copy-start(bf16[1,1,313600]{2,1,0:T(2,128)(2,1)} %copy-done.1) | copy-start | bytes 1881604
  199.9 21.5 %copy-start = (bf16[1,1,313600]{2,1,0:T(2,128)(2,1)S(1)}, bf16[1,1,313600]{2,1,0:T(2,128)(2,1)}, u32[]{:S(2)}) copy-start(bf16[1,1,313600]{2,1,0:T(2,128)(2,1)} %param.11) | copy-start | bytes 1881604
  199.9 147.1 %all-gather.3.cloned.1.call-start = ((), (), s32[]{:S(2)}) async-start(), calls=%async_computation.1 | async-start | bytes 2654208 | tf_op jit(solution)/shard_map/all_gather | solution.py:24
  221.1 141.0 %all-gather.5.cloned.1.call-start = ((), (), s32[]{:S(2)}) async-start(), calls=%async_computation.2 | async-start | bytes 15482880 | tf_op jit(solution)/shard_map/all_gather | solution.py:80
  302.6 1.1 copy-start.6
  302.6 5.1 %copy-start.9 = (bf16[1,4,32,2240]{3,2,1,0:T(8,128)(2,1)S(1)}, bf16[1,4,32,2240]{3,2,1,0:T(8,128)(2,1)}, u32[]{:S(2)}) copy-start(bf16[1,4,32,2240]{3,2,1,0:T(8,128)(2,1)} %param.7) | copy-start | bytes 1720324
  347.0 10.0 %copy-start.7 = (f32[1,70,1024]{1,2,0:T(8,128)S(1)}, f32[1,70,1024]{1,2,0:T(8,128)}, u32[]{:S(2)}) copy-start(f32[1,70,1024]{1,2,0:T(8,128)} %all-reduce.2.cloned.1.call-done) | copy-start | bytes 860164
  359.0 1.3 copy-start.8
  360.3 1.5 copy-start.11
Sparse Core Ops, SparseCore 0:
  200.0 19.0 all-reduce.1
  221.3 53.0 all-gather.2
  302.8 22.7 all-gather.4
